TPU v7x, 32 devices: a whole 2x2x4 slice. The times are simulated.
32 devices in a mesh: orow: 8 (over z, x), ocol: 4 (over y, core).
Axes of the slice: x: 2, y: 2, z: 4, core: 2. Of those that a mesh axis runs over, the one named last changes fastest.
Arguments:
- integrals: bfloat16 [2304, 16, 384], P('ocol', 'orow'), may hold values from -0.29882812 to 0.29882812
- occ_count: int32 [8], replicated, may hold values from 1 to 2
- occ_energy: float32 [16], replicated, may hold values from -2 to -0.5
- vir_energy: float32 [384], replicated, may hold values from 0.3 to 2.5
- task_iblock: int32 [32, 1], replicated, may hold values from 0 to 7; in each aligned block of 32 rows (0 to 31, 32 to 63, ...) at most 8 rows name the same one
- task_jblock: int32 [32], replicated, may hold values from 0 to 7
Outputs:
- gamma_out: float32 [2304, 16, 384], P('ocol', 'orow')
- density: float32 [384, 384], replicated
Inputs may be any that keep to these rules, and one draw needn't show every extreme that they name: `task_iblock`: no first block is named by more than 8 tasks, and some first block by exactly 8.
All inputs are finite; a program needn't handle non-finite values.
Results may differ from a plain program's by a relative error of at most 0.0019.
Values may be sent and summed in bfloat16 or wider, within the bound.
A program may use at most 128 MiB of HBM per device.

v0:
```python
import jax
import jax.numpy as jnp
from jax import lax
from jax.sharding import PartitionSpec as P


def make_amplitudes(k_total, i_energy, j_energy, vir_energy, usable):
    slots = k_total.shape[0]
    orbitals = i_energy.shape[1]
    virtuals = vir_energy.shape[0]
    k_grid = k_total.reshape(slots, orbitals, virtuals, orbitals, virtuals)
    denominator = (
        i_energy[:, :, None, None, None]
        + j_energy[:, None, None, :, None]
        - vir_energy[None, None, :, None, None]
        - vir_energy[None, None, None, None, :]
    )
    values = (2.0 * k_grid - jnp.swapaxes(k_grid, 2, 4)) / denominator
    values = values * usable[:, None, None, None, None]
    return values.astype(jnp.bfloat16).reshape(slots, orbitals * virtuals, orbitals * virtuals)


def local(integrals, occ_count, occ_energy, vir_energy, task_iblock, task_jblock):
    aux_local = integrals.shape[0]
    orbitals = integrals.shape[1]
    virtuals = integrals.shape[2]
    span = orbitals * virtuals
    block_total = lax.axis_size("orow")
    col_total = lax.axis_size("ocol")
    my_row = lax.axis_index("orow")
    my_col = lax.axis_index("ocol")
    active = jnp.arange(orbitals) < occ_count[my_row]
    masked = integrals * active.astype(jnp.bfloat16)[None, :, None]
    gathered = lax.all_gather(masked, "orow", axis=1, tiled=True)
    flat_blocks = gathered.reshape(aux_local, block_total, span)
    first_list = task_iblock[:, 0]
    task_total = first_list.shape[0]
    per_row = task_total // block_total
    task_ids = my_row * per_row + jnp.arange(per_row)
    i_block = first_list[task_ids]
    j_block = task_jblock[task_ids]
    usable = jnp.ones((per_row,), jnp.float32)
    energy_grid = occ_energy.reshape(block_total, orbitals)
    i_rows = jnp.take(flat_blocks, i_block, axis=1)
    j_rows = jnp.take(flat_blocks, j_block, axis=1)
    k_partial = jnp.einsum("psx,psy->sxy", i_rows, j_rows, preferred_element_type=jnp.float32)
    slots = k_partial.shape[0]
    i_energy = energy_grid[i_block]
    j_energy = energy_grid[j_block]
    k_total = lax.psum(k_partial, "ocol")
    amplitudes = make_amplitudes(k_total, i_energy, j_energy, vir_energy, usable)
    gamma_i = jnp.einsum("sxy,psy->psx", amplitudes, j_rows, preferred_element_type=jnp.float32)
    gamma_j = jnp.einsum("sxy,psx->psy", amplitudes, i_rows, preferred_element_type=jnp.float32)
    slice_width = span // col_total
    amp_grid = amplitudes.reshape(slots, orbitals, virtuals, span)
    column_part = lax.dynamic_slice_in_dim(amp_grid, my_col * slice_width, slice_width, 3)
    dens_part = jnp.einsum(
        "siaw,sibw->ab", column_part, column_part, preferred_element_type=jnp.float32
    )
    block_ids = jnp.arange(block_total)
    i_onehot = (i_block[:, None] == block_ids[None, :]).astype(jnp.float32)
    j_onehot = (j_block[:, None] == block_ids[None, :]).astype(jnp.float32)
    buffer = jnp.einsum(
        "sk,psx->pkx", i_onehot, gamma_i, precision=lax.Precision.HIGHEST
    ) + jnp.einsum("sk,psx->pkx", j_onehot, gamma_j, precision=lax.Precision.HIGHEST)
    owned = lax.psum_scatter(buffer, "orow", scatter_dimension=1, tiled=True)
    gamma_out = owned.reshape(aux_local, orbitals, virtuals)
    density = lax.psum(dens_part, ("orow", "ocol")) / task_total
    return (gamma_out, density)


def solution(mesh):
    return jax.shard_map(
        local,
        mesh=mesh,
        in_specs=(P("ocol", "orow", None), P(), P(), P(), P(), P()),
        out_specs=(P("ocol", "orow", None), P()),
        check_vma=False,
    )
```

profile of v0, /device:TPU:0, one launch (start us, length us, event | category | flops | bytes accessed | tf_op | source)
XLA Modules:
  0.0 801.5 jit_solution(11271543090973514411)
XLA Ops:
  7.2 0.0 copy-start
  7.2 0.0 all-gather.2.cloned.1.call-start
  7.2 1.2 dynamic_slice.6
  8.5 0.6 compare_convert_fusion
  9.1 2.3 copy_multiply_fusion
  11.4 0.0 all-gather.2.cloned.1.call-update
  11.4 0.0 all-reduce.3.cloned.1.call-start
  11.5 0.0 copy-done
  11.5 0.6 gather_fusion.1
  12.1 0.0 copy-start.4
  12.1 1.3 gather_fusion
  13.4 0.0 copy-start.6
  13.5 0.5 compare_and_fusion
  14.0 108.6 %all-gather.2.cloned.1.call-done = bf16[576,16,384]{2,0,1:T(8,128)(2,1)} async-done(((bf16[576,2,384]{2,0,1:T(8,128)(2,1)}), bf16[576,16,384]{2,0,1:T(8,128)(2,1)}) %all-gather.2.cloned.1.call-update) | async-done | bytes 7077904 | tf_op jit(solution)/shard_map/all_gather | solution.py:34
  122.6 10.1 %copy.40 = bf16[576,16,384]{2,1,0:T(8,128)(2,1)} copy(bf16[576,16,384]{2,0,1:T(8,128)(2,1)} %all-gather.2.cloned.1.call-done) | data formatting | bytes 14155776 | tf_op jit(solution)/shard_map/all_gather | solution.py:34
  132.7 0.0 copy-done.4
  132.7 11.3 %reshape.89 = bf16[576,8,768]{2,1,0:T(8,128)(2,1)} reshape(bf16[576,16,384]{2,1,0:T(8,128)(2,1)} %copy.40) | data formatting | bytes 14155776 | tf_op jit(solution)/shard_map/reshape | solution.py:35
  144.0 7.4 copy.41
  151.4 5.6 gather_fusion.5
  157.0 3.8 gather_fusion.4
  160.8 0.0 copy-done.9
  160.8 0.0 copy-done.11
  160.8 9.3 %fusion.7 = f32[4,768,768]{2,1,0:T(8,128)} fusion(bf16[4,576,768]{2,1,0:T(8,128)(2,1)S(1)} %gather_fusion.4, pred[4]{0:T(512)(128)(4,1)S(1)} %get-tuple-element.4, bf16[4,576,768]{2,1,0:T(8,128)(2,1)} %gather_fusion.5, pred[4]{0:T(512)(128)(4,1)S(1)} %copy-done.11), kind=kOutput, calls=%fused_computation.15 | convolution fusion | flops 2721447936 | bytes 16515080 | tf_op jit(solution)/shard_map/psx,psy->sxy/dot_general | solution.py:46
  170.1 12.5 %reshape.90 = f32[4,2,384,2,384]{4,3,2,1,0:T(2,128)} reshape(f32[4,768,768]{2,1,0:T(8,128)} %fusion.7) | data formatting | bytes 18874368 | tf_op jit(solution)/shard_map/reshape | solution.py:11
  182.6 14.8 %copy.43 = f32[4,2,384,2,384]{2,4,3,1,0:T(8,128)} copy(f32[4,2,384,2,384]{4,3,2,1,0:T(2,128)} %reshape.90) | data formatting | bytes 18874368 | tf_op jit(solution)/shard_map/reshape | solution.py:11
  197.4 0.0 all-reduce.3.cloned.1.call-update
  197.4 0.5 all-reduce.5.cloned.1.call-start
  198.0 0.1 copy-done.8
  198.1 0.1 reshape.91
  198.2 0.0 copy-done.6
  198.2 0.6 gather_fusion.3
  198.7 0.6 fusion.26
  199.3 0.6 pad_clamp_fusion.1
  199.9 0.7 gather_fusion.2
  200.6 0.1 broadcast_add_fusion
  200.7 0.0 copy-done.3
  200.7 0.7 broadcast_subtract_fusion
  201.4 164.2 %all-reduce.3.cloned.1.call-done = f32[4,2,384,2,384]{2,4,3,1,0:T(8,128)} async-done(((f32[4,2,384,2,384]{2,4,3,1,0:T(8,128)}), f32[4,2,384,2,384]{2,4,3,1,0:T(8,128)}) %all-reduce.3.cloned.1.call-update) | async-done | bytes 9437200 | tf_op jit(solution)/shard_map/psum | solution.py:50
  365.6 9.6 %copy.44 = f32[4,2,384,2,384]{4,2,3,1,0:T(8,128)} copy(f32[4,2,384,2,384]{2,4,3,1,0:T(8,128)} %all-reduce.3.cloned.1.call-done) | data formatting | bytes 18874368 | tf_op jit(solution)/shard_map/psum | solution.py:50
  375.2 9.6 %fusion.1 = bf16[4,2,384,2,384]{4,2,3,1,0:T(8,128)(2,1)} fusion(f32[4,2,384,2,384]{2,4,3,1,0:T(8,128)} %all-reduce.3.cloned.1.call-done, f32[4,2,384,2,384]{4,2,3,1,0:T(8,128)} %copy.44, f32[384]{0:T(512)S(1)} %copy-done.3, f32[4,2,384,2]{2,3,1,0:T(2,128)} %broadcast_subtract_fusion), kind=kLoop, calls=%fused_computation.9 | loop fusion | flops 11796480 | bytes 23619072 | tf_op jit(solution)/shard_map/convert_element_type | solution.py:20
  384.8 6.7 copy.52
  391.5 9.3 %copy.45 = bf16[4,2,384,2,384]{4,3,2,1,0:T(2,128)(2,1)} copy(bf16[4,2,384,2,384]{4,2,3,1,0:T(8,128)(2,1)} %fusion.1) | data formatting | bytes 9437184 | tf_op jit(solution)/shard_map/convert_element_type | solution.py:20
  400.8 11.3 %reshape.92 = bf16[4,768,768]{2,1,0:T(8,128)(2,1)} reshape(bf16[4,2,384,2,384]{4,3,2,1,0:T(2,128)(2,1)} %copy.45) | data formatting | bytes 9437184 | tf_op jit(solution)/shard_map/reshape | solution.py:20
  412.1 0.0 copy-done.12
  412.1 9.4 %fusion.15 = f32[576,4,768]{2,0,1:T(8,128)} fusion(bf16[4,768,768]{2,1,0:T(8,128)(2,1)} %reshape.92, bf16[4,576,768]{2,1,0:T(8,128)(2,1)} %gather_fusion.5, pred[4]{0:T(512)(128)(4,1)S(1)} %copy-done.12), kind=kOutput, calls=%fused_computation.23 | convolution fusion | flops 2719678464 | bytes 15335428 | tf_op jit(solution)/shard_map/sxy,psx->psy/dot_general | solution.py:53
  421.5 0.0 copy-done.2
  421.5 0.0 copy-done.10
  421.5 5.2 fusion.12
  426.8 3.3 convolution_bitcast_fusion
  430.0 0.0 all-reduce.5.cloned.1.call-update
  430.1 0.0 copy-start.7
  430.1 0.0 reduce-scatter.2.cloned.1.call-start
  430.1 0.0 copy-done.5
  430.1 14.4 %fusion.3 = f32[576,768,8]{1,2,0:T(8,128)S(1)} fusion(f32[576,4,768]{2,0,1:T(8,128)} %fusion.12, s32[4]{0:T(128)S(1)} %copy-done.5), kind=kOutput, calls=%fused_computation.11 | convolution fusion | flops 169869344 | bytes 21233680 | tf_op jit(solution)/shard_map/sk,psx->pkx/dot_general | solution.py:63
  444.6 0.0 copy-done.7
  444.6 18.4 %add_bitcast_fusion = f32[576,8,768]{2,1,0:T(8,128)} fusion(f32[576,768,8]{1,2,0:T(8,128)S(1)} %fusion.3, f32[576,4,768]{2,0,1:T(8,128)} %fusion.15, s32[4]{0:T(128)S(1)} %copy-done.7), kind=kOutput, calls=%fused_computation.6 | convolution fusion | flops 173408288 | bytes 35389456 | tf_op jit(solution)/shard_map/sk,psx->pkx/dot_general | solution.py:65
  462.9 14.7 %copy.48 = f32[576,8,768]{2,0,1:T(8,128)} copy(f32[576,8,768]{2,1,0:T(8,128)} %add_bitcast_fusion) | data formatting | bytes 28311552 | tf_op jit(solution)/shard_map/add | solution.py:63
  477.6 0.0 reduce-scatter.2.cloned.1.call-update
  477.6 0.0 copy-start.1
  477.6 80.9 %all-reduce.5.cloned.1.call-done = f32[384,384]{1,0:T(8,128)} async-done(((f32[384,384]{1,0:T(8,128)}), f32[384,384]{1,0:T(8,128)}) %all-reduce.5.cloned.1.call-update) | async-done | bytes 589840 | tf_op jit(solution)/shard_map/psum | solution.py:68
  558.5 1.9 broadcast_multiply_fusion
  560.5 231.3 %reduce-scatter.2.cloned.1.call-done = f32[576,1,768]{2,0,1:T(8,128)} async-done(((f32[576,8,768]{2,0,1:T(8,128)}), f32[576,1,768]{2,0,1:T(8,128)}) %reduce-scatter.2.cloned.1.call-update) | async-done | bytes 1769488 | tf_op jit(solution)/shard_map/reduce_scatter | solution.py:66
  791.7 3.1 reshape.93
  794.8 0.0 copy-done.1
  (16 shorter events, 0.1 us)
Async XLA Ops:
  7.2 4.3 copy-start
  7.2 115.4 %all-gather.2.cloned.1.call-start = ((), (), s32[]{:S(2)}) async-start(), calls=%async_computation.1 | async-start | bytes 7962624 | tf_op jit(solution)/shard_map/all_gather | solution.py:34
  11.4 354.2 %all-reduce.3.cloned.1.call-start = ((), (), s32[]{:S(2)}) async-start(), calls=%async_computation.2 | async-start | bytes 18874368 | tf_op jit(solution)/shard_map/psum | solution.py:50
  12.1 120.6 %copy-start.4 = (s32[4]{0:T(128)}, s32[4]{0:T(128)S(1)}, u32[]{:S(2)}) copy-start(s32[4]{0:T(128)S(1)} %gather_fusion.1) | copy-start | bytes 52
  13.4 184.7 %copy-start.6 = (s32[4]{0:T(128)}, s32[4]{0:T(128)S(1)}, u32[]{:S(2)}) copy-start(s32[4]{0:T(128)S(1)} %gather_fusion) | copy-start | bytes 52
  14.0 146.8 %copy-start.9 = (pred[4]{0:T(512)(128)(4,1)}, pred[4]{0:T(512)(128)(4,1)S(1)}, u32[]{:S(2)}) copy-start(pred[4]{0:T(512)(128)(4,1)S(1)} %get-tuple-element.4) | copy-start | bytes 16
  157.0 3.8 copy-start.11
  197.4 0.7 copy-start.8
  197.4 3.3 copy-start.3
  197.4 361.1 %all-reduce.5.cloned.1.call-start = ((), (), s32[]{:S(2)}) async-start(), calls=%async_computation.4 | async-start | bytes 1179648 | tf_op jit(solution)/shard_map/psum | solution.py:68
  400.8 11.4 %copy-start.12 = (pred[4]{0:T(512)(128)(4,1)S(1)}, pred[4]{0:T(512)(128)(4,1)}, u32[]{:S(2)}) copy-start(pred[4]{0:T(512)(128)(4,1)} %get-tuple-element.3) | copy-start | bytes 16
  412.1 9.4 %copy-start.2 = (bf16[4,768,768]{2,1,0:T(8,128)(2,1)S(1)}, bf16[4,768,768]{2,1,0:T(8,128)(2,1)}, u32[]{:S(2)}) copy-start(bf16[4,768,768]{2,1,0:T(8,128)(2,1)} %reshape.92) | copy-start | bytes 14155780
  412.1 9.4 %copy-start.10 = (pred[4]{0:T(512)(128)(4,1)S(1)}, pred[4]{0:T(512)(128)(4,1)}, u32[]{:S(2)}) copy-start(pred[4]{0:T(512)(128)(4,1)} %copy-done.9) | copy-start | bytes 16
  421.5 8.6 %copy-start.5 = (s32[4]{0:T(128)S(1)}, s32[4]{0:T(128)}, u32[]{:S(2)}) copy-start(s32[4]{0:T(128)} %copy-done.4) | copy-start | bytes 52
  430.1 14.5 %copy-start.7 = (s32[4]{0:T(128)S(1)}, s32[4]{0:T(128)}, u32[]{:S(2)}) copy-start(s32[4]{0:T(128)} %copy-done.6) | copy-start | bytes 52
  430.1 361.6 %reduce-scatter.2.cloned.1.call-start = ((), (), s32[]{:S(2)}) async-start(), calls=%async_computation.3 | async-start | bytes 15925248 | tf_op jit(solution)/shard_map/reduce_scatter | solution.py:66
  477.6 317.1 %copy-start.1 = (s32[32,1]{0,1:T(1,128)S(1)}, s32[32,1]{0,1:T(1,128)}, u32[]{:S(2)}) copy-start(s32[32,1]{0,1:T(1,128)} %param.12) | copy-start | bytes 388
Sparse Core Ops, SparseCore 0:
  11.5 111.0 all-gather.1
  197.6 167.9 all-reduce.2
  430.2 128.3 all-reduce.4
  562.0 229.6 reduce-scatter.1
where the time goes:
time: 811 us; the launch traced here: 802 us
  waiting for transfers between devices  585 us (72%)
  local copies, waits for them, and re-layouts  125 us (15%)
  matrix products  60 us (7%)
  other arithmetic  16.9 us (2%)
  between operations  14.2 us (2%)
    reduce_scatter x1, waiting for transfers between devices, local(): owned = lax.psum_scatter(buffer, 'orow', scatter_dimension=1, tiled=True)  231 us
    psum x1, waiting for transfers between devices, local(): k_total = lax.psum(k_partial, 'ocol')  164 us
    all_gather x1, waiting for transfers between devices, local(): gathered = lax.all_gather(masked, 'orow', axis=1, tiled=True)  109 us
    psum x1, waiting for transfers between devices, local(): density = lax.psum(dens_part, ('orow', 'ocol')) / task_total  80.9 us
    reshape x2, local copies, waits for them, and re-layouts, make_amplitudes(): k_grid = k_total.reshape(slots, orbitals, virtuals, orbitals, virtuals)  27.3 us
    reshape x2, local copies, waits for them, and re-layouts, local(): flat_blocks = gathered.reshape(aux_local, block_total, span)  18.6 us
    dot_general x1, matrix products, local(): jnp.einsum('sk,psx->pkx', j_onehot, gamma_j, precision=lax.Precision.HIGH...  18.4 us
  transfers between devices with their start and end apart: 4, of which 4 were waited for; matrix products, arithmetic and copies ran while one was open for 7% of the time, Pallas kernels for 0%

commit v1 on v0

--- a/solution.py
+++ b/solution.py
@@ -2,6 +2,11 @@
 import jax.numpy as jnp
 from jax import lax
 from jax.sharding import PartitionSpec as P
+
+
+def by_each_axis(x, axis_one, axis_two):
+    inner = lax.psum(x, axis_one)
+    return lax.psum(inner, axis_two)
 
 
 def make_amplitudes(k_total, i_energy, j_energy, vir_energy, usable):
@@ -65,7 +70,7 @@
     ) + jnp.einsum("sk,psx->pkx", j_onehot, gamma_j, precision=lax.Precision.HIGHEST)
     owned = lax.psum_scatter(buffer, "orow", scatter_dimension=1, tiled=True)
     gamma_out = owned.reshape(aux_local, orbitals, virtuals)
-    density = lax.psum(dens_part, ("orow", "ocol")) / task_total
+    density = by_each_axis(dens_part, "ocol", "orow") / task_total
     return (gamma_out, density)
 
 

time: 811 us -> 792 us (0.977)
  waiting for transfers between devices: 585 us -> 561 us
    psum x1 -> x2, waiting for transfers between devices: 80.9 us -> 58 us  [the longest x1 41.5 us: by_each_axis(): return lax.psum(inner, axis_two)]
  transfers between devices with their start and end apart: 4 -> 5, of which waited for: 4 -> 5; matrix products, arithmetic and copies ran while one was open for 7% -> 8% of each run, Pallas kernels for 0% -> 0%
where the time goes in v1:
time: 792 us; the launch traced here: 782 us
  waiting for transfers between devices  561 us (71%)
  local copies, waits for them, and re-layouts  125 us (16%)
  matrix products  64.9 us (8%)
  other arithmetic  16.9 us (2%)
  between operations  14.2 us (2%)
    reduce_scatter x1, waiting for transfers between devices, local(): owned = lax.psum_scatter(buffer, 'orow', scatter_dimension=1, tiled=True)  230 us
    psum x1, waiting for transfers between devices, local(): k_total = lax.psum(k_partial, 'ocol')  164 us
    all_gather x1, waiting for transfers between devices, local(): gathered = lax.all_gather(masked, 'orow', axis=1, tiled=True)  109 us
    psum x1, waiting for transfers between devices, by_each_axis(): return lax.psum(inner, axis_two)  41.5 us
    reshape x2, local copies, waits for them, and re-layouts, make_amplitudes(): k_grid = k_total.reshape(slots, orbitals, virtuals, orbitals, virtuals)  27.3 us
    dot_general x1, matrix products, local(): jnp.einsum('sk,psx->pkx', j_onehot, gamma_j, precision=lax.Precision.HIGH...  20.2 us
    reshape x2, local copies, waits for them, and re-layouts, local(): flat_blocks = gathered.reshape(aux_local, block_total, span)  18.6 us
    dot_general x1, matrix products, local(): jnp.einsum('sk,psx->pkx', i_onehot, gamma_i, precision=lax.Precision.HIGH...  17.5 us
  transfers between devices with their start and end apart: 5, of which 5 were waited for; matrix products, arithmetic and copies ran while one was open for 8% of the time, Pallas kernels for 0%

profile of v1, /device:TPU:0, one launch (start us, length us, event | category | flops | bytes accessed | tf_op | source)
XLA Modules:
  0.0 782.3 jit_solution(8443943927913695250)
XLA Ops:
  7.2 0.0 copy-start
  7.2 0.0 all-gather.2.cloned.1.call-start
  7.2 1.2 dynamic_slice.6
  8.5 0.6 compare_convert_fusion
  9.1 2.3 copy_multiply_fusion
  11.4 0.0 all-gather.2.cloned.1.call-update
  11.4 0.0 all-reduce.4.cloned.1.call-start
  11.5 0.0 copy-done
  11.5 0.6 gather_fusion.1
  12.1 1.3 gather_fusion
  13.5 0.5 compare_and_fusion
  14.0 108.6 %all-gather.2.cloned.1.call-done = bf16[576,16,384]{2,0,1:T(8,128)(2,1)} async-done(((bf16[576,2,384]{2,0,1:T(8,128)(2,1)}), bf16[576,16,384]{2,0,1:T(8,128)(2,1)}) %all-gather.2.cloned.1.call-update) | async-done | bytes 7077904 | tf_op jit(solution)/shard_map/all_gather | solution.py:39
  122.6 10.1 %copy.40 = bf16[576,16,384]{2,1,0:T(8,128)(2,1)} copy(bf16[576,16,384]{2,0,1:T(8,128)(2,1)} %all-gather.2.cloned.1.call-done) | data formatting | bytes 14155776 | tf_op jit(solution)/shard_map/all_gather | solution.py:39
  132.7 0.0 copy-done.4
  132.7 11.3 %reshape.89 = bf16[576,8,768]{2,1,0:T(8,128)(2,1)} reshape(bf16[576,16,384]{2,1,0:T(8,128)(2,1)} %copy.40) | data formatting | bytes 14155776 | tf_op jit(solution)/shard_map/reshape | solution.py:40
  144.0 7.4 copy.41
  151.4 5.6 gather_fusion.5
  157.0 3.8 gather_fusion.4
  160.8 0.0 copy-done.9
  160.8 0.0 copy-done.11
  160.8 9.3 %fusion.7 = f32[4,768,768]{2,1,0:T(8,128)} fusion(bf16[4,576,768]{2,1,0:T(8,128)(2,1)S(1)} %gather_fusion.4, pred[4]{0:T(512)(128)(4,1)S(1)} %get-tuple-element.4, bf16[4,576,768]{2,1,0:T(8,128)(2,1)} %gather_fusion.5, pred[4]{0:T(512)(128)(4,1)S(1)} %copy-done.11), kind=kOutput, calls=%fused_computation.15 | convolution fusion | flops 2721447936 | bytes 16515080 | tf_op jit(solution)/shard_map/psx,psy->sxy/dot_general | solution.py:51
  170.1 12.5 %reshape.90 = f32[4,2,384,2,384]{4,3,2,1,0:T(2,128)} reshape(f32[4,768,768]{2,1,0:T(8,128)} %fusion.7) | data formatting | bytes 18874368 | tf_op jit(solution)/shard_map/reshape | solution.py:16
  182.6 14.8 %copy.43 = f32[4,2,384,2,384]{2,4,3,1,0:T(8,128)} copy(f32[4,2,384,2,384]{4,3,2,1,0:T(2,128)} %reshape.90) | data formatting | bytes 18874368 | tf_op jit(solution)/shard_map/reshape | solution.py:16
  197.4 0.0 all-reduce.4.cloned.1.call-update
  197.4 0.5 all-reduce.6.cloned.1.call-start
  198.0 0.1 copy-done.8
  198.1 0.1 reshape.91
  198.2 0.0 copy-done.6
  198.2 0.6 gather_fusion.3
  198.7 0.6 fusion.26
  199.3 0.6 pad_clamp_fusion.1
  199.9 0.7 gather_fusion.2
  200.6 0.1 broadcast_add_fusion
  200.7 0.0 copy-done.3
  200.7 0.7 broadcast_subtract_fusion
  201.4 164.2 %all-reduce.4.cloned.1.call-done = f32[4,2,384,2,384]{2,4,3,1,0:T(8,128)} async-done(((f32[4,2,384,2,384]{2,4,3,1,0:T(8,128)}), f32[4,2,384,2,384]{2,4,3,1,0:T(8,128)}) %all-reduce.4.cloned.1.call-update) | async-done | bytes 9437200 | tf_op jit(solution)/shard_map/psum | solution.py:55
  365.6 9.6 %copy.44 = f32[4,2,384,2,384]{4,2,3,1,0:T(8,128)} copy(f32[4,2,384,2,384]{2,4,3,1,0:T(8,128)} %all-reduce.4.cloned.1.call-done) | data formatting | bytes 18874368 | tf_op jit(solution)/shard_map/psum | solution.py:55
  375.2 9.6 %fusion.1 = bf16[4,2,384,2,384]{4,2,3,1,0:T(8,128)(2,1)} fusion(f32[4,2,384,2,384]{2,4,3,1,0:T(8,128)} %all-reduce.4.cloned.1.call-done, f32[4,2,384,2,384]{4,2,3,1,0:T(8,128)} %copy.44, f32[384]{0:T(512)S(1)} %copy-done.3, f32[4,2,384,2]{2,3,1,0:T(2,128)} %broadcast_subtract_fusion), kind=kLoop, calls=%fused_computation.9 | loop fusion | flops 11796480 | bytes 23619072 | tf_op jit(solution)/shard_map/convert_element_type | solution.py:25
  384.8 6.7 copy.52
  391.5 9.3 %copy.45 = bf16[4,2,384,2,384]{4,3,2,1,0:T(2,128)(2,1)} copy(bf16[4,2,384,2,384]{4,2,3,1,0:T(8,128)(2,1)} %fusion.1) | data formatting | bytes 9437184 | tf_op jit(solution)/shard_map/convert_element_type | solution.py:25
  400.8 11.3 %reshape.92 = bf16[4,768,768]{2,1,0:T(8,128)(2,1)} reshape(bf16[4,2,384,2,384]{4,3,2,1,0:T(2,128)(2,1)} %copy.45) | data formatting | bytes 9437184 | tf_op jit(solution)/shard_map/reshape | solution.py:25
  412.1 0.0 copy-done.12
  412.1 9.4 %fusion.15 = f32[576,4,768]{2,0,1:T(8,128)} fusion(bf16[4,768,768]{2,1,0:T(8,128)(2,1)} %reshape.92, bf16[4,576,768]{2,1,0:T(8,128)(2,1)} %gather_fusion.5, pred[4]{0:T(512)(128)(4,1)S(1)} %copy-done.12), kind=kOutput, calls=%fused_computation.23 | convolution fusion | flops 2719678464 | bytes 15335428 | tf_op jit(solution)/shard_map/sxy,psx->psy/dot_general | solution.py:58
  421.5 0.0 copy-done.2
  421.5 0.0 copy-done.10
  421.5 5.2 fusion.12
  426.8 3.3 convolution_bitcast_fusion
  430.0 0.0 all-reduce.6.cloned.1.call-update
  430.1 0.0 copy-start.7
  430.1 0.0 all-reduce.8.cloned.1.call-start
  430.1 0.0 copy-done.5
  430.1 17.5 %fusion.3 = f32[576,768,8]{1,2,0:T(8,128)} fusion(f32[576,4,768]{2,0,1:T(8,128)} %fusion.12, s32[4]{0:T(128)S(1)} %copy-done.5), kind=kOutput, calls=%fused_computation.11 | convolution fusion | flops 169869344 | bytes 21233680 | tf_op jit(solution)/shard_map/sk,psx->pkx/dot_general | solution.py:68
  447.6 16.5 %all-reduce.6.cloned.1.call-done = f32[384,384]{1,0:T(8,128)} async-done(((f32[384,384]{1,0:T(8,128)}), f32[384,384]{1,0:T(8,128)}) %all-reduce.6.cloned.1.call-update) | async-done | bytes 589840 | tf_op jit(solution)/shard_map/psum | solution.py:8
  464.1 0.0 all-reduce.8.cloned.1.call-update
  464.1 0.0 reduce-scatter.2.cloned.1.call-start
  464.2 20.2 %add_bitcast_fusion = f32[576,8,768]{2,1,0:T(8,128)} fusion(f32[576,768,8]{1,2,0:T(8,128)} %fusion.3, f32[576,4,768]{2,0,1:T(8,128)} %fusion.15, s32[4]{0:T(128)S(1)} %copy-done.7), kind=kOutput, calls=%fused_computation.6 | convolution fusion | flops 173408288 | bytes 35389456 | tf_op jit(solution)/shard_map/sk,psx->pkx/dot_general | solution.py:70
  484.4 14.7 %copy.48 = f32[576,8,768]{2,0,1:T(8,128)} copy(f32[576,8,768]{2,1,0:T(8,128)} %add_bitcast_fusion) | data formatting | bytes 28311552 | tf_op jit(solution)/shard_map/add | solution.py:68
  499.1 0.0 reduce-scatter.2.cloned.1.call-update
  499.1 0.0 copy-start.1
  499.1 41.5 %all-reduce.8.cloned.1.call-done = f32[384,384]{1,0:T(8,128)} async-done(((f32[384,384]{1,0:T(8,128)}), f32[384,384]{1,0:T(8,128)}) %all-reduce.8.cloned.1.call-update) | async-done | bytes 589840 | tf_op jit(solution)/shard_map/psum | solution.py:9
  540.6 1.9 broadcast_multiply_fusion
  542.5 229.9 %reduce-scatter.2.cloned.1.call-done = f32[576,1,768]{2,0,1:T(8,128)} async-done(((f32[576,8,768]{2,0,1:T(8,128)}), f32[576,1,768]{2,0,1:T(8,128)}) %reduce-scatter.2.cloned.1.call-update) | async-done | bytes 1769488 | tf_op jit(solution)/shard_map/reduce_scatter | solution.py:71
  772.5 3.1 reshape.93
  775.5 0.0 copy-done.1
  (19 shorter events, 0.1 us)
Async XLA Ops:
  7.2 4.3 copy-start
  7.2 115.4 %all-gather.2.cloned.1.call-start = ((), (), s32[]{:S(2)}) async-start(), calls=%async_computation.1 | async-start | bytes 7962624 | tf_op jit(solution)/shard_map/all_gather | solution.py:39
  11.4 354.2 %all-reduce.4.cloned.1.call-start = ((), (), s32[]{:S(2)}) async-start(), calls=%async_computation.2 | async-start | bytes 18874368 | tf_op jit(solution)/shard_map/psum | solution.py:55
  12.1 120.6 %copy-start.4 = (s32[4]{0:T(128)}, s32[4]{0:T(128)S(1)}, u32[]{:S(2)}) copy-start(s32[4]{0:T(128)S(1)} %gather_fusion.1) | copy-start | bytes 52
  13.4 184.7 %copy-start.6 = (s32[4]{0:T(128)}, s32[4]{0:T(128)S(1)}, u32[]{:S(2)}) copy-start(s32[4]{0:T(128)S(1)} %gather_fusion) | copy-start | bytes 52
  14.0 146.8 %copy-start.9 = (pred[4]{0:T(512)(128)(4,1)}, pred[4]{0:T(512)(128)(4,1)S(1)}, u32[]{:S(2)}) copy-start(pred[4]{0:T(512)(128)(4,1)S(1)} %get-tuple-element.4) | copy-start | bytes 16
  157.0 3.8 copy-start.11
  197.4 0.7 copy-start.8
  197.4 3.3 copy-start.3
  197.4 266.7 %all-reduce.6.cloned.1.call-start = ((), (), s32[]{:S(2)}) async-start(), calls=%async_computation.4 | async-start | bytes 1179648 | tf_op jit(solution)/shard_map/psum | solution.py:8
  400.8 11.4 %copy-start.12 = (pred[4]{0:T(512)(128)(4,1)S(1)}, pred[4]{0:T(512)(128)(4,1)}, u32[]{:S(2)}) copy-start(pred[4]{0:T(512)(128)(4,1)} %get-tuple-element.3) | copy-start | bytes 16
  412.1 9.4 %copy-start.2 = (bf16[4,768,768]{2,1,0:T(8,128)(2,1)S(1)}, bf16[4,768,768]{2,1,0:T(8,128)(2,1)}, u32[]{:S(2)}) copy-start(bf16[4,768,768]{2,1,0:T(8,128)(2,1)} %reshape.92) | copy-start | bytes 14155780
  412.1 9.4 %copy-start.10 = (pred[4]{0:T(512)(128)(4,1)S(1)}, pred[4]{0:T(512)(128)(4,1)}, u32[]{:S(2)}) copy-start(pred[4]{0:T(512)(128)(4,1)} %copy-done.9) | copy-start | bytes 16
  421.5 8.6 %copy-start.5 = (s32[4]{0:T(128)S(1)}, s32[4]{0:T(128)}, u32[]{:S(2)}) copy-start(s32[4]{0:T(128)} %copy-done.4) | copy-start | bytes 52
  430.1 34.1 %copy-start.7 = (s32[4]{0:T(128)S(1)}, s32[4]{0:T(128)}, u32[]{:S(2)}) copy-start(s32[4]{0:T(128)} %copy-done.6) | copy-start | bytes 52
  430.1 110.6 %all-reduce.8.cloned.1.call-start = ((), (), s32[]{:S(2)}) async-start(), calls=%async_computation.5 | async-start | bytes 1179648 | tf_op jit(solution)/shard_map/psum | solution.py:9
  464.1 308.3 %reduce-scatter.2.cloned.1.call-start = ((), (), s32[]{:S(2)}) async-start(), calls=%async_computation.3 | async-start | bytes 15925248 | tf_op jit(solution)/shard_map/reduce_scatter | solution.py:71
  499.1 276.5 %copy-start.1 = (s32[32,1]{0,1:T(1,128)S(1)}, s32[32,1]{0,1:T(1,128)}, u32[]{:S(2)}) copy-start(s32[32,1]{0,1:T(1,128)} %param.12) | copy-start | bytes 388
Sparse Core Ops, SparseCore 0:
  11.5 111.0 all-gather.1
  197.6 167.9 all-reduce.3
  430.2 33.8 all-reduce.5
  467.3 73.2 all-reduce.7
  544.1 228.3 reduce-scatter.1
